TPU v7x, 32 devices: a whole 2x2x4 slice. The times are simulated.
32 devices in a mesh: grp: 2 (over y), vec: 4 (over z), occ: 2 (over x), wlk: 2 (over core).
Axes of the slice: x: 2, y: 2, z: 4, core: 2. Of those that a mesh axis runs over, the one named last changes fastest.
Arguments:
- chol_half: bfloat16 [256, 256, 2048], P(('grp', 'vec'), 'occ'), parts along dimension 0, may hold values from -0.046875 to 0.046875
- theta: bfloat16 [8, 2048, 256], P(('grp', 'wlk'), 'vec', 'occ'), parts along dimension 0, may hold values from -6 to 6
Outputs:
- theta_grad: float32 [8, 2048, 256], P(('grp', 'wlk'), 'vec', 'occ'), parts along dimension 0
There are 2 independent parts, one for each index of `grp`. A program takes and returns all parts, laid end to end along the dimension named above; each array names one. Nothing has to cross between parts.
All inputs are finite; a program needn't handle non-finite values.
Results may differ from a plain program's by a relative error of at most 0.0042.
Values may be sent and summed in bfloat16 or wider, within the bound.
No kernel may reach another device: no remote copies, remote signals or barrier semaphores. Data moves between devices by JAX's collectives and lax.ppermute only.
A program may use at most 64 MiB of HBM per device.

v0:
```python
import jax
import jax.numpy as jnp
from jax import lax
from jax.sharding import PartitionSpec as P


def on_device(chol_half, theta):
    widened = lax.all_gather(theta, "occ", axis=2, tiled=True)
    factor_rows = chol_half
    amplitude_sums = jnp.einsum(
        "gip,wpj->wgij",
        factor_rows,
        lax.all_gather(widened, "vec", axis=1, tiled=True),
        preferred_element_type=jnp.float32,
    )
    amplitudes = amplitude_sums.astype(jnp.bfloat16)
    swapped = lax.all_to_all(amplitudes, "occ", split_axis=3, concat_axis=2, tiled=True)
    factor_rows = chol_half
    summed_rows = lax.psum_scatter(
        jnp.einsum("gap,wgba->pwb", factor_rows, swapped, preferred_element_type=jnp.float32),
        "vec",
        scatter_dimension=0,
        tiled=True,
    )
    owned = lax.psum_scatter(summed_rows, "occ", scatter_dimension=2, tiled=True)
    return -jnp.transpose(owned, (1, 0, 2))


def solution(mesh):
    placed = (P(("grp", "vec"), "occ", None), P(("grp", "wlk"), "vec", "occ"))
    return jax.shard_map(
        on_device,
        mesh=mesh,
        in_specs=placed,
        out_specs=P(("grp", "wlk"), "vec", "occ"),
        check_vma=False,
    )
```

profile of v0, /device:TPU:0, one launch (start us, length us, event | category | flops | bytes accessed | tf_op | source)
XLA Modules:
  0.0 259.8 jit_solution(8337746905256795681)
XLA Ops:
  6.5 0.0 all-gather.2.cloned.1.call-start
  6.5 1.1 copy.6
  7.6 10.0 %all_gather.6 = bf16[2,512,256]{1,2,0:T(8,128)(2,1)} all-gather(bf16[2,512,128]{1,2,0:T(8,128)(2,1)S(1)} %copy.6), channel_id=1, replica_groups=mesh['grp'=2,'vec'=4,'occ'=2,'wlk'=2] {'occ'}, dimensions={2}, use_global_device_ids=true | all-gather | bytes 786432 | tf_op jit(solution)/shard_map/all_gather | solution.py:8
  17.7 0.0 all-gather.2.cloned.1.call-update
  17.7 0.0 reduce-scatter.3.cloned.1.call-start
  17.7 47.3 %all-gather.2.cloned.1.call-done = bf16[2,2048,256]{1,2,0:T(8,128)(2,1)} async-done(((bf16[2,512,256]{1,2,0:T(8,128)(2,1)}), bf16[2,2048,256]{1,2,0:T(8,128)(2,1)}) %all-gather.2.cloned.1.call-update) | async-done | bytes 2097168 | tf_op jit(solution)/shard_map/all_gather | solution.py:13
  65.0 12.4 %convert_bitcast_fusion = bf16[2,32,128,256]{2,3,1,0:T(8,128)(2,1)S(1)} fusion(bf16[32,128,2048]{2,1,0:T(8,128)(2,1)} %param.2, bf16[2,2048,256]{1,2,0:T(8,128)(2,1)} %all-gather.2.cloned.1.call-done), kind=kOutput, calls=%fused_computation.4 | convolution fusion | flops 8592031744 | bytes 23068672 | tf_op jit(solution)/shard_map/gip,wpj->wgij/dot_general | solution.py:10
  77.4 2.7 %copy.7 = bf16[2,32,128,256]{2,1,0,3:T(8,128)(2,1)S(1)} copy(bf16[2,32,128,256]{2,3,1,0:T(8,128)(2,1)S(1)} %convert_bitcast_fusion) | data formatting | bytes 8388608 | tf_op jit(solution)/shard_map/convert_element_type | solution.py:16
  80.1 51.1 %all_to_all.18 = bf16[2,32,128,256]{2,1,0,3:T(8,128)(2,1)} all-to-all(bf16[2,32,128,256]{2,1,0,3:T(8,128)(2,1)S(1)} %copy.7), channel_id=1, replica_groups=mesh['grp'=2,'vec'=4,'occ'=2,'wlk'=2] {'occ'}, dimensions={3} | all-to-all | bytes 8388608 | tf_op jit(solution)/shard_map/all_to_all | solution.py:17
  131.3 7.5 %copy.8 = bf16[2,32,128,2,128]{4,2,3,1,0:T(8,128)(2,1)} copy(bf16[2,32,128,2,128]{2,1,0,4,3:T(8,128)(2,1)} %bitcast.28) | data formatting | bytes 8388608 | tf_op jit(solution)/shard_map/all_to_all | solution.py:17
  138.8 14.1 %fusion.4 = f32[2048,2,256]{0,2,1:T(8,128)} fusion(bf16[2,32,256,128]{3,2,1,0:T(8,128)(2,1)} %bitcast.29, bf16[32,128,2048]{2,1,0:T(8,128)(2,1)} %param.2), kind=kOutput, calls=%fused_computation.5 | convolution fusion | flops 8589934592 | bytes 25165824 | tf_op jit(solution)/shard_map/gap,wgba->pwb/dot_general | solution.py:20
  152.9 0.0 reduce-scatter.3.cloned.1.call-update
  152.9 0.0 reduce-scatter.5.cloned.1.call-start
  153.0 75.0 %reduce-scatter.3.cloned.1.call-done = f32[512,2,256]{0,2,1:T(8,128)} async-done(((f32[2048,2,256]{0,2,1:T(8,128)}), f32[512,2,256]{0,2,1:T(8,128)}) %reduce-scatter.3.cloned.1.call-update) | async-done | bytes 1048592 | tf_op jit(solution)/shard_map/reduce_scatter | solution.py:19
  228.0 0.0 reduce-scatter.5.cloned.1.call-update
  228.0 23.1 %reduce-scatter.5.cloned.1.call-done = f32[512,2,128]{0,2,1:T(8,128)} async-done(((f32[512,2,256]{0,2,1:T(8,128)}), f32[512,2,128]{0,2,1:T(8,128)}) %reduce-scatter.5.cloned.1.call-update) | async-done | bytes 524304 | tf_op jit(solution)/shard_map/reduce_scatter | solution.py:25
  251.2 1.1 negate_bitcast_fusion
  252.3 1.0 copy.9
Async XLA Ops:
  6.5 58.5 %all-gather.2.cloned.1.call-start = ((), (), s32[]{:S(2)}) async-start(), calls=%async_computation.3 | async-start | bytes 2621440 | tf_op jit(solution)/shard_map/all_gather | solution.py:13
  17.7 210.3 %reduce-scatter.3.cloned.1.call-start = ((), (), s32[]{:S(2)}) async-start(), calls=%async_computation.4 | async-start | bytes 5242880 | tf_op jit(solution)/shard_map/reduce_scatter | solution.py:19
  152.9 98.2 %reduce-scatter.5.cloned.1.call-start = ((), (), s32[]{:S(2)}) async-start(), calls=%async_computation.5 | async-start | bytes 1572864 | tf_op jit(solution)/shard_map/reduce_scatter | solution.py:25
Sparse Core Ops, SparseCore 0:
  17.8 47.1 all-gather.1
  153.0 74.9 reduce-scatter.2
  230.2 20.8 reduce-scatter.4
where the time goes:
time: 260 us
  waiting for transfers between devices  145 us (56%)
  blocking collectives  61.2 us (24%)
  matrix products  26.5 us (10%)
  between operations  13.1 us (5%)
  local copies, waits for them, and re-layouts  12.3 us (5%)
    reduce_scatter x1, waiting for transfers between devices, on_device(): lax.psum_scatter(jnp.einsum('gap,wgba->pwb', factor_rows, swapped, prefer...  75 us
    all_to_all x1, blocking collectives, on_device(): lax.all_to_all(amplitudes, 'occ', split_axis=3, concat_axis=2, tiled=True)  51.1 us
    all_gather x1, waiting for transfers between devices, on_device(): lax.all_gather(widened, 'vec', axis=1, tiled=True)  47.3 us
    reduce_scatter x1, waiting for transfers between devices, on_device(): lax.psum_scatter(summed_rows, 'occ', scatter_dimension=2, tiled=True)  23.1 us
    dot_general x1, matrix products, on_device(): jnp.einsum('gap,wgba->pwb', factor_rows, swapped, preferred_element_type=...  14.1 us
    dot_general x1, matrix products, on_device(): jnp.einsum('gip,wpj->wgij', factor_rows, lax.all_gather(widened, 'vec', a...  12.4 us
    all_gather x1, blocking collectives, on_device(): widened = lax.all_gather(theta, 'occ', axis=2, tiled=True)  10 us
    all_to_all x1, local copies, waits for them, and re-layouts, on_device(): lax.all_to_all(amplitudes, 'occ', split_axis=3, concat_axis=2, tiled=True)  7.48 us
  transfers between devices with their start and end apart: 3, of which 3 were waited for; matrix products, arithmetic and copies ran while one was open for 0% of the time, Pallas kernels for 0%

commit v1 on v0

--- a/solution.py
+++ b/solution.py
@@ -2,6 +2,11 @@
 import jax.numpy as jnp
 from jax import lax
 from jax.sharding import PartitionSpec as P
+
+
+def all_by_exchange(x, axis, dim):
+    sent = jnp.stack([x] * lax.axis_size(axis))
+    return jnp.concatenate(lax.all_to_all(sent, axis, 0, 0), axis=dim)
 
 
 def on_device(chol_half, theta):
@@ -10,7 +15,7 @@
     amplitude_sums = jnp.einsum(
         "gip,wpj->wgij",
         factor_rows,
-        lax.all_gather(widened, "vec", axis=1, tiled=True),
+        all_by_exchange(widened, "vec", 1),
         preferred_element_type=jnp.float32,
     )
     amplitudes = amplitude_sums.astype(jnp.bfloat16)

time: 260 us -> 269 us (1.035)
  blocking collectives: 61.2 us -> 112 us
  waiting for transfers between devices: 145 us -> 99 us
  local copies, waits for them, and re-layouts: 12.3 us -> 16 us
    all_to_all x0 -> x1, blocking collectives: none -> 52.2 us  [all_by_exchange(): return jnp.concatenate(lax.all_to_all(sent, axis, 0, 0), axis=dim)]
    all_gather x1 -> x0, waiting for transfers between devices: 47.3 us -> none  [on_device(): lax.all_gather(widened, 'vec', axis=1, tiled=True)]
    reshape x0 -> x2, local copies, waits for them, and re-layouts: none -> 4.42 us  [all_by_exchange(): return jnp.concatenate(lax.all_to_all(sent, axis, 0, 0), axis=dim)]
  transfers between devices with their start and end apart: 3 -> 2, of which waited for: 3 -> 2; matrix products, arithmetic and copies ran while one was open for 0% -> 0% of each run, Pallas kernels for 0% -> 0%
where the time goes in v1:
time: 269 us
  blocking collectives  112 us (42%)
  waiting for transfers between devices  99 us (37%)
  matrix products  26.6 us (10%)
  local copies, waits for them, and re-layouts  16 us (6%)
  between operations  13.4 us (5%)
    reduce_scatter x1, waiting for transfers between devices, on_device(): lax.psum_scatter(jnp.einsum('gap,wgba->pwb', factor_rows, swapped, prefer...  75.8 us
    all_to_all x1, blocking collectives, all_by_exchange(): return jnp.concatenate(lax.all_to_all(sent, axis, 0, 0), axis=dim)  52.2 us
    all_to_all x1, blocking collectives, on_device(): lax.all_to_all(amplitudes, 'occ', split_axis=3, concat_axis=2, tiled=True)  50.1 us
    reduce_scatter x1, waiting for transfers between devices, on_device(): lax.psum_scatter(summed_rows, 'occ', scatter_dimension=2, tiled=True)  23.2 us
    dot_general x1, matrix products, on_device(): jnp.einsum('gap,wgba->pwb', factor_rows, swapped, preferred_element_type=...  14.2 us
    dot_general x1, matrix products, on_device(): jnp.einsum('gip,wpj->wgij', factor_rows, all_by_exchange(widened, 'vec',...  12.4 us
    all_gather x1, blocking collectives, on_device(): widened = lax.all_gather(theta, 'occ', axis=2, tiled=True)  10.2 us
    all_to_all x1, local copies, waits for them, and re-layouts, on_device(): lax.all_to_all(amplitudes, 'occ', split_axis=3, concat_axis=2, tiled=True)  7.51 us
  transfers between devices with their start and end apart: 2, of which 2 were waited for; matrix products, arithmetic and copies ran while one was open for 0% of the time, Pallas kernels for 0%

profile of v1, /device:TPU:0, one launch (start us, length us, event | category | flops | bytes accessed | tf_op | source)
XLA Modules:
  0.0 268.6 jit_solution(12080509854704249515)
XLA Ops:
  6.5 0.0 reduce-scatter.3.cloned.1.call-start
  6.5 10.2 %all_gather.3 = bf16[2,512,256]{2,1,0:T(8,128)(2,1)S(1)} all-gather(bf16[2,512,128]{2,1,0:T(8,128)(2,1)} %param.3), channel_id=1, replica_groups=mesh['grp'=2,'vec'=4,'occ'=2,'wlk'=2] {'occ'}, dimensions={2}, use_global_device_ids=true | all-gather | bytes 786432 | tf_op jit(solution)/shard_map/all_gather | solution.py:13
  16.7 0.2 copy.6
  17.0 0.2 stack.2
  17.1 52.2 %all_to_all.23 = bf16[4,2,512,256]{2,3,1,0:T(8,128)(2,1)S(1)} all-to-all(bf16[4,2,512,256]{2,3,1,0:T(8,128)(2,1)S(1)} %stack.2), channel_id=1, replica_groups=mesh['grp'=2,'vec'=4,'occ'=2,'wlk'=2] {'vec'}, dimensions={0} | all-to-all | bytes 4194304 | tf_op jit(solution)/shard_map/all_to_all | solution.py:9
  69.3 1.6 copy.7
  71.0 2.8 %reshape.10 = bf16[2,2048,256,1]{1,2,0,3:T(8,128)(2,1)} reshape(bf16[2,4,512,256]{2,1,3,0:T(4,128)(2,1)S(1)} %copy.7) | data formatting | bytes 4194304 | tf_op jit(solution)/shard_map/reshape | solution.py:9
  73.8 12.4 %convert_bitcast_fusion = bf16[2,32,128,256]{2,3,1,0:T(8,128)(2,1)S(1)} fusion(bf16[32,128,2048]{2,1,0:T(8,128)(2,1)} %param.2, bf16[2,2048,256,1]{1,2,0,3:T(8,128)(2,1)} %reshape.10), kind=kOutput, calls=%fused_computation.4 | convolution fusion | flops 8592031744 | bytes 23068672 | tf_op jit(solution)/shard_map/gip,wpj->wgij/dot_general | solution.py:15
  86.2 2.7 %copy.8 = bf16[2,32,128,256]{2,1,0,3:T(8,128)(2,1)S(1)} copy(bf16[2,32,128,256]{2,3,1,0:T(8,128)(2,1)S(1)} %convert_bitcast_fusion) | data formatting | bytes 8388608 | tf_op jit(solution)/shard_map/convert_element_type | solution.py:21
  88.9 50.1 %all_to_all.24 = bf16[2,32,128,256]{2,1,0,3:T(8,128)(2,1)} all-to-all(bf16[2,32,128,256]{2,1,0,3:T(8,128)(2,1)S(1)} %copy.8), channel_id=1, replica_groups=mesh['grp'=2,'vec'=4,'occ'=2,'wlk'=2] {'occ'}, dimensions={3} | all-to-all | bytes 8388608 | tf_op jit(solution)/shard_map/all_to_all | solution.py:22
  139.0 7.5 %copy.9 = bf16[2,32,128,2,128]{4,2,3,1,0:T(8,128)(2,1)} copy(bf16[2,32,128,2,128]{2,1,0,4,3:T(8,128)(2,1)} %bitcast.29) | data formatting | bytes 8388608 | tf_op jit(solution)/shard_map/all_to_all | solution.py:22
  146.5 14.2 %fusion.4 = f32[2048,2,256]{0,2,1:T(8,128)} fusion(bf16[2,32,256,128]{3,2,1,0:T(8,128)(2,1)} %bitcast.31, bf16[32,128,2048]{2,1,0:T(8,128)(2,1)} %param.2), kind=kOutput, calls=%fused_computation.5 | convolution fusion | flops 8589934592 | bytes 25165824 | tf_op jit(solution)/shard_map/gap,wgba->pwb/dot_general | solution.py:25
  160.7 0.0 reduce-scatter.3.cloned.1.call-update
  160.7 0.0 reduce-scatter.5.cloned.1.call-start
  160.7 75.8 %reduce-scatter.3.cloned.1.call-done = f32[512,2,256]{0,2,1:T(8,128)} async-done(((f32[2048,2,256]{0,2,1:T(8,128)}), f32[512,2,256]{0,2,1:T(8,128)}) %reduce-scatter.3.cloned.1.call-update) | async-done | bytes 1048592 | tf_op jit(solution)/shard_map/reduce_scatter | solution.py:24
  236.5 0.0 reduce-scatter.5.cloned.1.call-update
  236.6 23.2 %reduce-scatter.5.cloned.1.call-done = f32[512,2,128]{0,2,1:T(8,128)} async-done(((f32[512,2,256]{0,2,1:T(8,128)}), f32[512,2,128]{0,2,1:T(8,128)}) %reduce-scatter.5.cloned.1.call-update) | async-done | bytes 524304 | tf_op jit(solution)/shard_map/reduce_scatter | solution.py:30
  259.7 1.1 negate_bitcast_fusion
  260.8 1.0 copy.10
Async XLA Ops:
  6.5 230.0 %reduce-scatter.3.cloned.1.call-start = ((), (), s32[]{:S(2)}) async-start(), calls=%async_computation.4 | async-start | bytes 5242880 | tf_op jit(solution)/shard_map/reduce_scatter | solution.py:24
  160.7 99.0 %reduce-scatter.5.cloned.1.call-start = ((), (), s32[]{:S(2)}) async-start(), calls=%async_computation.5 | async-start | bytes 1572864 | tf_op jit(solution)/shard_map/reduce_scatter | solution.py:30
Sparse Core Ops, SparseCore 0:
  160.8 75.6 reduce-scatter.2
  238.8 20.8 reduce-scatter.4
